TPU v7x, 32 devices: a whole 2x2x4 slice. The times are simulated.
32 devices in a mesh: dp: 4 (over y, x), tensor: 8 (over z, core).
Axes of the slice: x: 2, y: 2, z: 4, core: 2. Of those that a mesh axis runs over, the one named last changes fastest.
Arguments:
- tokens: bfloat16 [2048, 8192], P('dp', 'tensor'), may hold values from -6 to 6
- cotangent: bfloat16 [2048, 8192], P('dp', 'tensor'), may hold values from -6 to 6
- w_first: bfloat16 [32, 256, 1024], P('tensor'), may hold values from -0.375 to 0.375
- w_second: bfloat16 [128, 256, 256], P('tensor'), may hold values from -0.375 to 0.375
- third_weight_blocks: bfloat16 [128, 256, 256], P('tensor'), may hold values from -0.375 to 0.375
- w_fourth: bfloat16 [32, 1024, 256], P('tensor'), may hold values from -0.1875 to 0.1875
Outputs:
- layer_out: bfloat16 [2048, 8192], P('dp', 'tensor')
- tokens_grad: bfloat16 [2048, 8192], P('dp', 'tensor')
- grad_first: float32 [32, 256, 1024], P('tensor')
- grad_second: float32 [128, 256, 256], P('tensor')
- grad_third: float32 [128, 256, 256], P('tensor')
- grad_fourth: float32 [32, 1024, 256], P('tensor')
All inputs are finite; a program needn't handle non-finite values.
Results may differ from a plain program's by a relative error of at most 0.0095.
Values may be sent and summed in bfloat16 or wider, within the bound.
No kernel may reach another device: no remote copies, remote signals or barrier semaphores. Data moves between devices by JAX's collectives and lax.ppermute only.
A program may use at most 128 MiB of HBM per device.

v0:
```python
import math
import jax
import jax.numpy as jnp
from jax import lax
from jax.sharding import PartitionSpec as P


def gelu_parts(value_in):
    cdf_part = 0.5 * (1.0 + lax.erf(value_in * 0.7071067811865476))
    slope_part = cdf_part + value_in * jnp.exp(-0.5 * value_in * value_in) * 0.3989422804014327
    return (value_in * cdf_part, slope_part)


def body(tokens, cotangent, w_first, w_second, third_weight_blocks, w_fourth):
    row_count = tokens.shape[0]
    width_dev = w_first.shape[0]
    block_width = w_first.shape[1]
    hidden_dev = w_second.shape[0]
    groups = lax.axis_size("tensor")
    in_blocks = width_dev * groups
    hid_blocks = hidden_dev * groups
    sub_width = block_width // in_blocks
    grad_scale = 1.0 / math.sqrt(row_count * lax.axis_size("dp"))
    inputs_view = tokens.reshape(row_count, width_dev, block_width)
    cot_view = cotangent.reshape(row_count, width_dev, block_width)
    first_factor_parts = w_first.reshape(width_dev, block_width, groups, hidden_dev, sub_width)
    first_view = w_first.reshape(width_dev, block_width, hid_blocks, sub_width)
    second_view = w_second.reshape(hidden_dev, in_blocks, sub_width, block_width)
    second_split = w_second.reshape(hidden_dev, groups, width_dev, sub_width, block_width)
    third_split = third_weight_blocks.reshape(hidden_dev, block_width, groups, width_dev, sub_width)
    fourth_view = w_fourth.reshape(width_dev, hid_blocks, sub_width, block_width)
    fourth_split = w_fourth.reshape(width_dev, groups, hidden_dev, sub_width, block_width)
    first_out = jnp.einsum(
        "tai,aigbc->gabct", inputs_view, first_factor_parts, preferred_element_type=jnp.float32
    )
    first_out = first_out.astype(jnp.bfloat16)
    received = lax.all_to_all(first_out, "tensor", split_axis=0, concat_axis=0, tiled=True)
    count = received.shape[4]
    flat_rows = received.reshape(in_blocks * hidden_dev, sub_width, count)
    spread = flat_rows
    count = flat_rows.shape[2]
    spread_view = flat_rows.reshape(in_blocks, hidden_dev, sub_width, count)
    pre_act = jnp.einsum(
        "abct,bacj->bjt", spread_view, second_view, preferred_element_type=jnp.float32
    )
    gelu_val, gelu_slope = gelu_parts(pre_act)
    activated = gelu_val.astype(jnp.bfloat16)
    third_factor_output = jnp.einsum(
        "bjt,bjgac->gbact", activated, third_split, preferred_element_type=jnp.float32
    )
    third_factor_output = third_factor_output.astype(jnp.bfloat16)
    received = lax.all_to_all(
        third_factor_output, "tensor", split_axis=0, concat_axis=0, tiled=True
    )
    count = received.shape[4]
    flat_rows = received.reshape(hid_blocks * width_dev, sub_width, count)
    merged = received.reshape(hid_blocks, width_dev, sub_width, count)
    out_part = jnp.einsum("bact,abck->akt", merged, fourth_view, preferred_element_type=jnp.float32)
    out_rows = out_part.astype(jnp.bfloat16)
    layer_out = jnp.transpose(out_rows, (2, 0, 1)).reshape(row_count, width_dev * block_width)
    third_grad = jnp.einsum(
        "tak,agbck->gbact", cot_view, fourth_split, preferred_element_type=jnp.float32
    )
    third_grad = third_grad.astype(jnp.bfloat16)
    collected_view = flat_rows.reshape(hid_blocks, width_dev, sub_width, row_count)
    grad_fourth = jnp.einsum(
        "bact,tak->abck", collected_view, cot_view, preferred_element_type=jnp.float32
    )
    grad_fourth = (grad_fourth * grad_scale).reshape(width_dev, hid_blocks * sub_width, block_width)
    returned = lax.all_to_all(third_grad, "tensor", split_axis=0, concat_axis=0, tiled=True)
    activation_gradient = jnp.einsum(
        "gbact,bjgac->bjt", returned, third_split, preferred_element_type=jnp.float32
    )
    pre_grad = (activation_gradient * gelu_slope).astype(jnp.bfloat16)
    grad_third = jnp.einsum(
        "bjt,gbact->bjgac", activated, returned, preferred_element_type=jnp.float32
    )
    grad_third = (grad_third * grad_scale).reshape(hidden_dev, block_width, block_width)
    first_grad = jnp.einsum(
        "bjt,bgacj->gbact", pre_grad, second_split, preferred_element_type=jnp.float32
    )
    first_grad = first_grad.astype(jnp.bfloat16)
    spread_view = spread.reshape(in_blocks, hidden_dev, sub_width, row_count)
    grad_second = jnp.einsum(
        "abct,bjt->bacj", spread_view, pre_grad, preferred_element_type=jnp.float32
    )
    grad_second = (grad_second * grad_scale).reshape(hidden_dev, block_width, block_width)
    back_first = lax.all_to_all(first_grad, "tensor", split_axis=0, concat_axis=0, tiled=True)
    back_view = back_first.reshape(hid_blocks, width_dev, sub_width, row_count)
    tokens_grad = jnp.einsum(
        "bact,aibc->tai", back_view, first_view, preferred_element_type=jnp.float32
    )
    tokens_grad = tokens_grad.astype(jnp.bfloat16).reshape(row_count, width_dev * block_width)
    grad_first = jnp.einsum(
        "tai,bact->aibc", inputs_view, back_view, preferred_element_type=jnp.float32
    )
    grad_first = (grad_first * grad_scale).reshape(width_dev, block_width, hid_blocks * sub_width)
    grad_first, grad_second, grad_third, grad_fourth = (
        lax.psum(grad_first.astype(jnp.bfloat16), "dp").astype(jnp.float32),
        lax.psum(grad_second.astype(jnp.bfloat16), "dp").astype(jnp.float32),
        lax.psum(grad_third.astype(jnp.bfloat16), "dp").astype(jnp.float32),
        lax.psum(grad_fourth.astype(jnp.bfloat16), "dp").astype(jnp.float32),
    )
    return (layer_out, tokens_grad, grad_first, grad_second, grad_third, grad_fourth)


def solution(mesh):
    return jax.shard_map(
        body,
        mesh=mesh,
        in_specs=(
            P("dp", "tensor"),
            P("dp", "tensor"),
            P("tensor", None, None),
            P("tensor", None, None),
            P("tensor", None, None),
            P("tensor", None, None),
        ),
        out_specs=(
            P("dp", "tensor"),
            P("dp", "tensor"),
            P("tensor", None, None),
            P("tensor", None, None),
            P("tensor", None, None),
            P("tensor", None, None),
        ),
        check_vma=False,
    )
```

profile of v0, /device:TPU:0, one launch (start us, length us, event | category | flops | bytes accessed | tf_op | source)
XLA Modules:
  0.0 628.3 jit_solution(12406556423778622042)
XLA Ops:
  7.2 0.0 copy-start
  7.2 2.0 reshape.60
  9.2 4.0 copy.64
  13.2 2.9 convert_bitcast_fusion.3
  16.1 2.5 copy.66
  18.5 6.3 %all-to-all-start = ((bf16[8,4,16,8,512]{4,3,2,1,0:T(8,128)(2,1)}), bf16[8,4,16,8,512]{4,3,2,1,0:T(8,128)(2,1)}, u32[]{:S(2)}, u32[]{:S(2)}) async-start(bf16[8,4,16,8,512]{4,3,2,1,0:T(8,128)(2,1)} %copy.66), calls=%async_computation | async-start | bytes 8388608 | tf_op jit(solution)/shard_map/all_to_all | solution.py:37
  24.9 2.6 reshape.67
  27.5 3.1 convert_bitcast_fusion.1
  30.6 2.5 copy.73
  33.1 85.9 %all-to-all-done = bf16[8,4,16,8,512]{4,3,2,1,0:T(8,128)(2,1)} async-done(((bf16[8,4,16,8,512]{4,3,2,1,0:T(8,128)(2,1)}), bf16[8,4,16,8,512]{4,3,2,1,0:T(8,128)(2,1)}, u32[]{:S(2)}, u32[]{:S(2)}) %all-to-all-start) | async-done | bytes 4194336 | tf_op jit(solution)/shard_map/all_to_all | solution.py:37
  119.0 4.6 all-to-all-start.2
  123.6 3.9 copy.68
  127.5 0.0 copy-done
  127.5 7.4 %fusion.9 = (bf16[16,256,512]{1,2,0:T(8,128)(2,1)}, f32[16,512,256,1]{2,1,0,3:T(8,128)}) fusion(bf16[32,16,8,512]{3,2,1,0:T(8,128)(2,1)} %bitcast.3, bf16[16,256,256]{2,1,0:T(8,128)(2,1)S(1)} %copy-done), kind=kOutput, calls=%fused_computation.12 | convolution fusion | flops 1084227584 | bytes 18874368 | tf_op jit(solution)/shard_map/abct,bacj->bjt/dot_general | solution.py:43
  134.9 82.7 %all-to-all-done.2 = bf16[8,16,4,8,512]{4,3,1,2,0:T(8,128)(2,1)} async-done(((bf16[8,16,4,8,512]{4,3,1,2,0:T(8,128)(2,1)}), bf16[8,16,4,8,512]{4,3,1,2,0:T(8,128)(2,1)}, u32[]{:S(2)}, u32[]{:S(2)}) %all-to-all-start.2) | async-done | bytes 4194336 | tf_op jit(solution)/shard_map/all_to_all | solution.py:70
  217.6 7.9 %fusion.5 = bf16[16,256,512]{1,2,0:T(8,128)(2,1)S(1)} fusion(f32[16,512,256,1]{2,1,0,3:T(8,128)} %get-tuple-element.29, bf16[8,16,4,8,512]{4,3,1,2,0:T(8,128)(2,1)} %all-to-all-done.2, bf16[16,256,8,4,8]{1,4,3,2,0:T(8,128)(2,1)} %bitcast.118), kind=kOutput, calls=%fused_computation.6 | convolution fusion | flops 1094713344 | bytes 18874368 | tf_op jit(solution)/shard_map/gbact,bjgac->bjt/dot_general | solution.py:71
  225.4 0.0 copy-start.5
  225.5 1.3 convert_bitcast_fusion
  226.8 0.7 copy-done.5
  227.5 2.5 copy.77
  230.0 0.0 copy-start.2
  230.0 4.9 all-to-all-start.3
  234.9 0.0 copy-done.2
  234.9 3.5 fusion.57
  238.4 0.7 convert_bitcast_fusion.2
  239.0 2.4 copy.70
  241.4 87.3 %all-to-all-done.3 = bf16[8,16,4,8,512]{4,3,2,1,0:T(8,128)(2,1)} async-done(((bf16[8,16,4,8,512]{4,3,2,1,0:T(8,128)(2,1)}), bf16[8,16,4,8,512]{4,3,2,1,0:T(8,128)(2,1)}, u32[]{:S(2)}, u32[]{:S(2)}) %all-to-all-start.3) | async-done | bytes 4194336 | tf_op jit(solution)/shard_map/all_to_all | solution.py:88
  328.7 4.5 all-to-all-start.1
  333.2 0.0 all-reduce.3.cloned.1.call-start
  333.3 4.7 multiply_convert_fusion.1
  338.0 2.5 copy.87
  340.5 6.0 fusion.33
  346.5 7.0 %fusion.32 = bf16[4,256,128,8]{1,2,3,0:T(8,128)(2,1)S(1)} fusion(bf16[128,4,8,512]{3,2,1,0:T(8,128)(2,1)} %bitcast.26, bf16[512,4,256,1]{2,1,0,3:T(4,128)(2,1)S(1)} %bitcast.114), kind=kOutput, calls=%fused_computation.35 | convolution fusion | flops 1075838976 | bytes 7340032 | tf_op jit(solution)/shard_map/tai,bact->aibc/dot_general | solution.py:94
  353.5 0.0 copy-start.4
  353.5 2.5 copy.162
  356.0 71.2 %all-to-all-done.1 = bf16[8,16,4,8,512]{4,3,2,1,0:T(8,128)(2,1)} async-done(((bf16[8,16,4,8,512]{4,3,2,1,0:T(8,128)(2,1)}), bf16[8,16,4,8,512]{4,3,2,1,0:T(8,128)(2,1)}, u32[]{:S(2)}, u32[]{:S(2)}) %all-to-all-start.1) | async-done | bytes 4194336 | tf_op jit(solution)/shard_map/all_to_all | solution.py:52
  427.2 0.0 copy-done.4
  427.2 7.2 %multiply_convert_fusion = bf16[4,128,8,256]{3,1,2,0:T(8,128)(2,1)S(1)} fusion(bf16[128,4,8,512]{3,2,1,0:T(8,128)(2,1)} %bitcast.12, bf16[512,4,256,1]{2,1,0,3:T(4,128)(2,1)S(1)} %bitcast.116), kind=kOutput, calls=%fused_computation.27 | convolution fusion | flops 1075838976 | bytes 7340032 | tf_op jit(solution)/shard_map/bact,tak->abck/dot_general | solution.py:66
  434.4 2.5 copy.161
  436.9 0.0 copy-start.3
  436.9 0.0 all-reduce.3.cloned.1.call-update
  437.0 1.6 copy-done.3
  438.5 3.5 bitcast_convert_fusion
  442.0 1.3 copy.92
  443.3 4.2 bitcast_convert_fusion.1
  447.5 1.3 copy.91
  448.8 160.9 %all-reduce.3.cloned.1.call-done = (bf16[4,256,1024]{1,2,0:T(8,128)(2,1)}, bf16[16,256,256]{2,1,0:T(8,128)(2,1)}, bf16[16,256,256]{2,1,0:T(8,128)(2,1)}, bf16[4,1024,256]{2,1,0:T(8,128)(2,1)}) async-done(((bf16[4,256,1024]{1,2,0:T(8,128)(2,1)}, bf16[16,256,256]{2,1,0:T(8,128)(2,1)}, bf16[16,256,256]{2,1,0:T(8,128)(2,1)}, bf16[4,1024,256]{2,1,0:T(8,128)(2,1)}), (bf16[4,256,1024]{1,2,0:T(8,128)(2,1)}, ...) | async-done | bytes 8388624 | tf_op jit(solution)/shard_map/psum | solution.py:99
  609.7 0.0 copy-start.8
  609.7 4.3 copy.93
  614.0 0.0 copy-start.7
  614.0 0.0 copy-done.8
  614.0 2.5 convert_element_type.102
  616.4 0.0 copy-start.6
  616.4 0.0 copy-done.7
  616.4 0.0 copy-start.1
  616.4 2.6 convert_element_type.105
  619.0 0.0 copy-done.6
  619.0 2.4 convert_element_type.108
  621.4 0.0 copy-done.1
Async XLA Ops:
  7.2 120.3 %copy-start = (bf16[16,256,256]{2,1,0:T(8,128)(2,1)S(1)}, bf16[16,256,256]{2,1,0:T(8,128)(2,1)}, u32[]{:S(2)}) copy-start(bf16[16,256,256]{2,1,0:T(8,128)(2,1)} %param.9) | copy-start | bytes 6291460
  18.5 100.4 %all-to-all-start = ((bf16[8,4,16,8,512]{4,3,2,1,0:T(8,128)(2,1)}), bf16[8,4,16,8,512]{4,3,2,1,0:T(8,128)(2,1)}, u32[]{:S(2)}, u32[]{:S(2)}) async-start(bf16[8,4,16,8,512]{4,3,2,1,0:T(8,128)(2,1)} %copy.66), calls=%async_computation | async-start | bytes 8388608 | tf_op jit(solution)/shard_map/all_to_all | solution.py:37
  119.0 98.6 %all-to-all-start.2 = ((bf16[8,16,4,8,512]{4,3,1,2,0:T(8,128)(2,1)}), bf16[8,16,4,8,512]{4,3,1,2,0:T(8,128)(2,1)}, u32[]{:S(2)}, u32[]{:S(2)}) async-start(bf16[8,16,4,8,512]{4,3,1,2,0:T(8,128)(2,1)} %copy.73), calls=%async_computation.2 | async-start | bytes 8388608 | tf_op jit(solution)/shard_map/all_to_all | solution.py:70
  225.4 2.0 copy-start.5
  230.0 4.9 copy-start.2
  230.0 98.7 %all-to-all-start.3 = ((bf16[8,16,4,8,512]{4,3,2,1,0:T(8,128)(2,1)}), bf16[8,16,4,8,512]{4,3,2,1,0:T(8,128)(2,1)}, u32[]{:S(2)}, u32[]{:S(2)}) async-start(bf16[8,16,4,8,512]{4,3,2,1,0:T(8,128)(2,1)} %copy.77), calls=%async_computation.3 | async-start | bytes 8388608 | tf_op jit(solution)/shard_map/all_to_all | solution.py:88
  328.7 98.6 %all-to-all-start.1 = ((bf16[8,16,4,8,512]{4,3,2,1,0:T(8,128)(2,1)}), bf16[8,16,4,8,512]{4,3,2,1,0:T(8,128)(2,1)}, u32[]{:S(2)}, u32[]{:S(2)}) async-start(bf16[8,16,4,8,512]{4,3,2,1,0:T(8,128)(2,1)} %copy.70), calls=%async_computation.1 | async-start | bytes 8388608 | tf_op jit(solution)/shard_map/all_to_all | solution.py:52
  333.2 276.5 %all-reduce.3.cloned.1.call-start = ((), (), s32[]{:S(2)}) async-start(), calls=%async_computation.4 | async-start | bytes 16777216 | tf_op jit(solution)/shard_map/psum | solution.py:99
  353.5 73.8 %copy-start.4 = (bf16[512,4,256]{2,1,0:T(4,128)(2,1)S(1)}, bf16[512,4,256]{2,1,0:T(4,128)(2,1)}, u32[]{:S(2)}) copy-start(bf16[512,4,256]{2,1,0:T(4,128)(2,1)} %reshape.67) | copy-start | bytes 3145732
  436.9 1.6 copy-start.3
  609.7 4.3 copy-start.8
  614.0 2.5 copy-start.7
  616.4 2.6 copy-start.6
  616.4 5.0 copy-start.1
Sparse Core Ops, SparseCore 0:
  437.1 172.5 all-reduce.2
where the time goes:
time: 629 us; the launch traced here: 628 us
  waiting for transfers between devices  488 us (78%)
  matrix products  58.6 us (9%)
  local copies, waits for them, and re-layouts  39 us (6%)
  starting transfers between devices  20.4 us (3%)
  between operations  14.2 us (2%)
  other arithmetic  8.08 us (1%)
    psum x1, waiting for transfers between devices, body(): lax.psum(grad_first.astype(jnp.bfloat16), 'dp').astype(jnp.float32)  161 us
    all_to_all x1, waiting for transfers between devices, body(): lax.all_to_all(first_grad, 'tensor', split_axis=0, concat_axis=0, tiled=T...  87.3 us
    all_to_all x1, waiting for transfers between devices, body(): lax.all_to_all(first_out, 'tensor', split_axis=0, concat_axis=0, tiled=True)  85.9 us
    all_to_all x1, waiting for transfers between devices, body(): lax.all_to_all(third_grad, 'tensor', split_axis=0, concat_axis=0, tiled=T...  82.7 us
    all_to_all x1, waiting for transfers between devices, body(): lax.all_to_all(third_factor_output, 'tensor', split_axis=0, concat_axis=0...  71.2 us
    unnamed x23, local copies, waits for them, and re-layouts  17 us
  transfers between devices with their start and end apart: 5, of which 5 were waited for; matrix products, arithmetic and copies ran while one was open for 9% of the time, Pallas kernels for 0%

commit v1 on v0

--- a/solution.py
+++ b/solution.py
@@ -1,8 +1,16 @@
+import functools
 import math
 import jax
 import jax.numpy as jnp
 from jax import lax
 from jax.sharding import PartitionSpec as P
+
+
+def part_table_on(local_array, net_axis):
+    return jnp.sum(lax.all_gather(local_array, net_axis), 0)
+
+
+remake_trees = functools.partial(part_table_on, net_axis="dp")
 
 
 def gelu_parts(value_in):
@@ -96,7 +104,7 @@
     )
     grad_first = (grad_first * grad_scale).reshape(width_dev, block_width, hid_blocks * sub_width)
     grad_first, grad_second, grad_third, grad_fourth = (
-        lax.psum(grad_first.astype(jnp.bfloat16), "dp").astype(jnp.float32),
+        remake_trees(grad_first.astype(jnp.bfloat16)).astype(jnp.float32),
         lax.psum(grad_second.astype(jnp.bfloat16), "dp").astype(jnp.float32),
         lax.psum(grad_third.astype(jnp.bfloat16), "dp").astype(jnp.float32),
         lax.psum(grad_fourth.astype(jnp.bfloat16), "dp").astype(jnp.float32),

time: 629 us -> 608 us (0.967); the launches traced: 628 us -> 600 us
  waiting for transfers between devices: 488 us -> 443 us
  other arithmetic: 8.08 us -> 17.2 us
  local copies, waits for them, and re-layouts: 39 us -> 47.9 us
    psum x1, waiting for transfers between devices: 161 us -> 47.5 us  [body(): lax.psum(grad_second.astype(jnp.bfloat16), 'dp').astype(jnp.float32)]
    all_gather x0 -> x1, waiting for transfers between devices: none -> 81 us  [part_table_on(): return jnp.sum(lax.all_gather(local_array, net_axis), 0)]
    all_to_all x1, waiting for transfers between devices: 87.3 us -> 68.1 us  [body(): lax.all_to_all(first_grad, 'tensor', split_axis=0, concat_axis=0, tiled=T...]
    reduce_sum x0 -> x1, other arithmetic: none -> 7.53 us  [part_table_on(): return jnp.sum(lax.all_gather(local_array, net_axis), 0)]
    all_to_all x1, waiting for transfers between devices: 71.2 us -> 77.7 us  [body(): lax.all_to_all(third_factor_output, 'tensor', split_axis=0, concat_axis=0...]
    unnamed x23 -> x20, local copies, waits for them, and re-layouts: 17 us -> 20 us
  transfers between devices with their start and end apart: 5 -> 6, of which waited for: 5 -> 6; matrix products, arithmetic and copies ran while one was open for 9% -> 16% of each run, Pallas kernels for 0% -> 0%
where the time goes in v1:
time: 608 us; the launch traced here: 600 us
  waiting for transfers between devices  443 us (73%)
  matrix products  57.2 us (9%)
  local copies, waits for them, and re-layouts  47.9 us (8%)
  starting transfers between devices  20.8 us (3%)
  other arithmetic  17.2 us (3%)
  between operations  14.4 us (2%)
    all_to_all x1, waiting for transfers between devices, body(): lax.all_to_all(first_out, 'tensor', split_axis=0, concat_axis=0, tiled=True)  85.9 us
    all_to_all x1, waiting for transfers between devices, body(): lax.all_to_all(third_grad, 'tensor', split_axis=0, concat_axis=0, tiled=T...  82.8 us
    all_gather x1, waiting for transfers between devices, part_table_on(): return jnp.sum(lax.all_gather(local_array, net_axis), 0)  81 us
    all_to_all x1, waiting for transfers between devices, body(): lax.all_to_all(third_factor_output, 'tensor', split_axis=0, concat_axis=0...  77.7 us
    all_to_all x1, waiting for transfers between devices, body(): lax.all_to_all(first_grad, 'tensor', split_axis=0, concat_axis=0, tiled=T...  68.1 us
    psum x1, waiting for transfers between devices, body(): lax.psum(grad_second.astype(jnp.bfloat16), 'dp').astype(jnp.float32)  47.5 us
    unnamed x20, local copies, waits for them, and re-layouts  20 us
  transfers between devices with their start and end apart: 6, of which 6 were waited for; matrix products, arithmetic and copies ran while one was open for 16% of the time, Pallas kernels for 0%

profile of v1, /device:TPU:0, one launch (start us, length us, event | category | flops | bytes accessed | tf_op | source)
XLA Modules:
  0.0 600.3 jit_solution(4896408687683124250)
XLA Ops:
  7.2 0.0 copy-start
  7.2 2.0 reshape.70
  9.2 4.0 copy.63
  13.2 2.9 convert_bitcast_fusion.3
  16.1 2.5 copy.65
  18.5 6.3 %all-to-all-start = ((bf16[8,4,16,8,512]{4,3,2,1,0:T(8,128)(2,1)}), bf16[8,4,16,8,512]{4,3,2,1,0:T(8,128)(2,1)}, u32[]{:S(2)}, u32[]{:S(2)}) async-start(bf16[8,4,16,8,512]{4,3,2,1,0:T(8,128)(2,1)} %copy.65), calls=%async_computation | async-start | bytes 8388608 | tf_op jit(solution)/shard_map/all_to_all | solution.py:45
  24.9 2.6 reshape.77
  27.5 3.1 convert_bitcast_fusion.1
  30.7 2.5 copy.72
  33.1 85.9 %all-to-all-done = bf16[8,4,16,8,512]{4,3,2,1,0:T(8,128)(2,1)} async-done(((bf16[8,4,16,8,512]{4,3,2,1,0:T(8,128)(2,1)}), bf16[8,4,16,8,512]{4,3,2,1,0:T(8,128)(2,1)}, u32[]{:S(2)}, u32[]{:S(2)}) %all-to-all-start) | async-done | bytes 4194336 | tf_op jit(solution)/shard_map/all_to_all | solution.py:45
  119.0 4.6 all-to-all-start.2
  123.6 0.0 copy-done
  123.6 0.0 copy-start.1
  123.6 6.2 %fusion.9 = (bf16[16,256,512]{1,2,0:T(8,128)(2,1)S(1)}, f32[16,512,256,1]{2,1,0,3:T(8,128)}) fusion(bf16[32,16,8,512]{3,2,1,0:T(8,128)(2,1)} %bitcast.3, bf16[16,256,256]{2,1,0:T(8,128)(2,1)S(1)} %copy-done), kind=kOutput, calls=%fused_computation.12 | convolution fusion | flops 1084227584 | bytes 18874368 | tf_op jit(solution)/shard_map/abct,bacj->bjt/dot_general | solution.py:51
  129.8 0.0 copy-start.2
  129.8 0.0 copy-done.1
  129.8 1.3 fusion.57
  131.1 0.7 copy-done.2
  131.8 0.7 convert_bitcast_fusion.2
  132.5 2.4 copy.69
  134.8 82.8 %all-to-all-done.2 = bf16[8,16,4,8,512]{4,3,1,2,0:T(8,128)(2,1)} async-done(((bf16[8,16,4,8,512]{4,3,1,2,0:T(8,128)(2,1)}), bf16[8,16,4,8,512]{4,3,1,2,0:T(8,128)(2,1)}, u32[]{:S(2)}, u32[]{:S(2)}) %all-to-all-start.2) | async-done | bytes 4194336 | tf_op jit(solution)/shard_map/all_to_all | solution.py:78
  217.6 5.1 all-to-all-start.1
  222.6 3.9 copy.67
  226.5 7.9 %fusion.5 = bf16[16,256,512]{1,2,0:T(8,128)(2,1)S(1)} fusion(f32[16,512,256,1]{2,1,0,3:T(8,128)} %get-tuple-element.28, bf16[8,16,4,8,512]{4,3,1,2,0:T(8,128)(2,1)} %all-to-all-done.2, bf16[16,256,8,4,8]{1,4,3,2,0:T(8,128)(2,1)} %bitcast.118), kind=kOutput, calls=%fused_computation.6 | convolution fusion | flops 1094713344 | bytes 18874368 | tf_op jit(solution)/shard_map/gbact,bjgac->bjt/dot_general | solution.py:79
  234.4 0.0 copy-start.4
  234.4 1.3 convert_bitcast_fusion
  235.8 0.7 copy-done.4
  236.4 2.5 copy.76
  238.9 77.7 %all-to-all-done.1 = bf16[8,16,4,8,512]{4,3,2,1,0:T(8,128)(2,1)} async-done(((bf16[8,16,4,8,512]{4,3,2,1,0:T(8,128)(2,1)}), bf16[8,16,4,8,512]{4,3,2,1,0:T(8,128)(2,1)}, u32[]{:S(2)}, u32[]{:S(2)}) %all-to-all-start.1) | async-done | bytes 4194336 | tf_op jit(solution)/shard_map/all_to_all | solution.py:60
  316.6 4.6 all-to-all-start.3
  321.2 0.0 all-reduce.3.cloned.1.call-start
  321.3 6.0 %multiply_convert_fusion.1 = bf16[16,256,8,4,8]{1,4,3,2,0:T(8,128)(2,1)} fusion(bf16[8,16,4,8,512]{4,3,1,2,0:T(8,128)(2,1)} %all-to-all-done.2, bf16[16,256,512]{1,2,0:T(8,128)(2,1)} %copy-done.2), kind=kOutput, calls=%fused_computation.28 | convolution fusion | flops 1075838976 | bytes 10485760 | tf_op jit(solution)/shard_map/bjt,gbact->bjgac/dot_general | solution.py:83
  327.3 4.0 copy.88
  331.3 0.0 copy-start.3
  331.3 6.2 %fusion.33 = bf16[16,256,256]{2,1,0:T(8,128)(2,1)} fusion(bf16[16,256,512]{1,2,0:T(8,128)(2,1)} %copy-done.4, bf16[32,16,8,512]{3,2,1,0:T(8,128)(2,1)} %bitcast.3), kind=kOutput, calls=%fused_computation.36 | convolution fusion | flops 1075838976 | bytes 10485760 | tf_op jit(solution)/shard_map/abct,bjt->bacj/dot_general | solution.py:92
  337.4 0.0 copy-done.3
  337.4 7.0 %multiply_convert_fusion = bf16[4,128,8,256]{3,1,2,0:T(8,128)(2,1)S(1)} fusion(bf16[128,4,8,512]{3,2,1,0:T(8,128)(2,1)} %bitcast.12, bf16[512,4,256,1]{2,1,0,3:T(4,128)(2,1)S(1)} %bitcast.116), kind=kOutput, calls=%fused_computation.27 | convolution fusion | flops 1075838976 | bytes 7340032 | tf_op jit(solution)/shard_map/bact,tak->abck/dot_general | solution.py:74
  344.4 2.5 copy.163
  346.9 0.0 all-reduce.3.cloned.1.call-update
  347.0 0.2 all-gather.2.cloned.1.call-start
  347.2 68.1 %all-to-all-done.3 = bf16[8,16,4,8,512]{4,3,2,1,0:T(8,128)(2,1)} async-done(((bf16[8,16,4,8,512]{4,3,2,1,0:T(8,128)(2,1)}), bf16[8,16,4,8,512]{4,3,2,1,0:T(8,128)(2,1)}, u32[]{:S(2)}, u32[]{:S(2)}) %all-to-all-start.3) | async-done | bytes 4194336 | tf_op jit(solution)/shard_map/all_to_all | solution.py:96
  415.2 7.0 %fusion.32 = bf16[4,256,128,8]{1,2,3,0:T(8,128)(2,1)S(1)} fusion(bf16[128,4,8,512]{3,2,1,0:T(8,128)(2,1)} %bitcast.26, bf16[512,4,256,1]{2,1,0,3:T(4,128)(2,1)S(1)} %bitcast.114), kind=kOutput, calls=%fused_computation.35 | convolution fusion | flops 1075838976 | bytes 7340032 | tf_op jit(solution)/shard_map/tai,bact->aibc/dot_general | solution.py:102
  422.2 2.5 copy.164
  424.7 4.4 copy.82
  429.1 0.0 all-gather.2.cloned.1.call-update
  429.2 4.2 bitcast_convert_fusion
  433.3 1.3 copy.93
  434.7 4.2 bitcast_convert_fusion.1
  438.8 1.3 copy.92
  440.1 47.5 %all-reduce.3.cloned.1.call-done = (bf16[16,256,256]{2,1,0:T(8,128)(2,1)}, bf16[16,256,256]{2,1,0:T(8,128)(2,1)}, bf16[4,1024,256]{2,1,0:T(8,128)(2,1)}) async-done(((bf16[16,256,256]{2,1,0:T(8,128)(2,1)}, bf16[16,256,256]{2,1,0:T(8,128)(2,1)}, bf16[4,1024,256]{2,1,0:T(8,128)(2,1)}), (bf16[16,256,256]{2,1,0:T(8,128)(2,1)}, bf16[16,256,256]{2,1,0:T(8,128)(2,1)}, ...) | async-done | bytes 6291472 | tf_op jit(solution)/shard_map/psum | solution.py:108
  487.6 0.0 copy-start.6
  487.6 4.2 convert_element_type.111
  491.8 0.0 copy-start.5
  491.8 0.0 copy-done.6
  491.8 2.5 convert_element_type.114
  494.3 0.0 copy-done.5
  494.3 2.4 convert_element_type.117
  496.6 81.0 %all-gather.2.cloned.1.call-done = bf16[4,4,256,1024]{3,2,1,0:T(8,128)(2,1)} async-done(((bf16[1,4,256,1024]{3,2,1,0:T(8,128)(2,1)}), bf16[4,4,256,1024]{3,2,1,0:T(8,128)(2,1)}) %all-gather.2.cloned.1.call-update) | async-done | bytes 8388624 | tf_op jit(solution)/shard_map/all_gather | solution.py:10
  577.7 7.5 %reduce_sum.12 = bf16[4,256,1024]{2,1,0:T(8,128)(2,1)} reduce(bf16[4,4,256,1024]{3,2,1,0:T(8,128)(2,1)} %all-gather.2.cloned.1.call-done, bf16[]{:T(256)} %constant.4.clone.1), dimensions={0}, to_apply=%region_0.0 | reduce | flops 3145728 | bytes 10485762 | tf_op jit(solution)/shard_map/reduce_sum | solution.py:10
  585.2 3.9 copy.118
  589.1 4.1 copy.94
Async XLA Ops:
  7.2 116.4 %copy-start = (bf16[16,256,256]{2,1,0:T(8,128)(2,1)S(1)}, bf16[16,256,256]{2,1,0:T(8,128)(2,1)}, u32[]{:S(2)}) copy-start(bf16[16,256,256]{2,1,0:T(8,128)(2,1)} %param.9) | copy-start | bytes 6291460
  18.5 100.4 %all-to-all-start = ((bf16[8,4,16,8,512]{4,3,2,1,0:T(8,128)(2,1)}), bf16[8,4,16,8,512]{4,3,2,1,0:T(8,128)(2,1)}, u32[]{:S(2)}, u32[]{:S(2)}) async-start(bf16[8,4,16,8,512]{4,3,2,1,0:T(8,128)(2,1)} %copy.65), calls=%async_computation | async-start | bytes 8388608 | tf_op jit(solution)/shard_map/all_to_all | solution.py:45
  119.0 98.6 %all-to-all-start.2 = ((bf16[8,16,4,8,512]{4,3,1,2,0:T(8,128)(2,1)}), bf16[8,16,4,8,512]{4,3,1,2,0:T(8,128)(2,1)}, u32[]{:S(2)}, u32[]{:S(2)}) async-start(bf16[8,16,4,8,512]{4,3,1,2,0:T(8,128)(2,1)} %copy.72), calls=%async_computation.2 | async-start | bytes 8388608 | tf_op jit(solution)/shard_map/all_to_all | solution.py:78
  123.6 6.2 %copy-start.1 = (bf16[16,256,256]{2,1,0:T(8,128)(2,1)S(1)}, bf16[16,256,256]{2,1,0:T(8,128)(2,1)}, u32[]{:S(2)}) copy-start(bf16[16,256,256]{2,1,0:T(8,128)(2,1)} %param.10) | copy-start | bytes 6291460
  129.8 2.0 copy-start.2
  217.6 99.1 %all-to-all-start.1 = ((bf16[8,16,4,8,512]{4,3,2,1,0:T(8,128)(2,1)}), bf16[8,16,4,8,512]{4,3,2,1,0:T(8,128)(2,1)}, u32[]{:S(2)}, u32[]{:S(2)}) async-start(bf16[8,16,4,8,512]{4,3,2,1,0:T(8,128)(2,1)} %copy.69), calls=%async_computation.1 | async-start | bytes 8388608 | tf_op jit(solution)/shard_map/all_to_all | solution.py:60
  234.4 2.0 copy-start.4
  316.6 98.6 %all-to-all-start.3 = ((bf16[8,16,4,8,512]{4,3,2,1,0:T(8,128)(2,1)}), bf16[8,16,4,8,512]{4,3,2,1,0:T(8,128)(2,1)}, u32[]{:S(2)}, u32[]{:S(2)}) async-start(bf16[8,16,4,8,512]{4,3,2,1,0:T(8,128)(2,1)} %copy.76), calls=%async_computation.3 | async-start | bytes 8388608 | tf_op jit(solution)/shard_map/all_to_all | solution.py:96
  321.2 166.4 %all-reduce.3.cloned.1.call-start = ((), (), s32[]{:S(2)}) async-start(), calls=%async_computation.5 | async-start | bytes 12582912 | tf_op jit(solution)/shard_map/psum | solution.py:108
  331.3 6.2 %copy-start.3 = (bf16[512,4,256]{2,1,0:T(4,128)(2,1)S(1)}, bf16[512,4,256]{2,1,0:T(4,128)(2,1)}, u32[]{:S(2)}) copy-start(bf16[512,4,256]{2,1,0:T(4,128)(2,1)} %reshape.77) | copy-start | bytes 3145732
  347.0 230.7 %all-gather.2.cloned.1.call-start = ((), (), s32[]{:S(2)}) async-start(), calls=%async_computation.4 | async-start | bytes 10485760 | tf_op jit(solution)/shard_map/all_gather | solution.py:10
  487.6 4.2 copy-start.6
  491.8 2.5 copy-start.5
Sparse Core Ops, SparseCore 0:
  347.1 140.4 all-reduce.2
  490.0 87.5 all-gather.1
